TPU v7x, 256 devices: a whole 4x4x8 slice. The times are simulated.
256 devices in a mesh: dp: 16 (over x, y), tensor: 8 (over z), side: 2 (over core).
Axes of the slice: x: 4, y: 4, z: 8, core: 2. Of those that a mesh axis runs over, the one named last changes fastest.
Arguments:
- q_new: bfloat16 [1024, 6144], P(('dp', 'side'), 'tensor'), may hold values from -6 to 6
- k_new: bfloat16 [1024, 1024], P(('dp', 'side'), 'tensor'), may hold values from -6 to 6
- v_new: bfloat16 [1024, 1024], P(('dp', 'side'), 'tensor'), may hold values from -6 to 6
- k_cache: bfloat16 [1024, 192, 1024], P(('dp', 'side'), None, 'tensor'), may hold values from -6 to 6
- v_cache: bfloat16 [1024, 192, 1024], P(('dp', 'side'), None, 'tensor'), may hold values from -6 to 6
- lengths: int32 [1024], P(('dp', 'side')), may hold values from 24 to 192, as said below
- attn_out_weight: bfloat16 [6144, 6144], P('tensor', ('dp', 'side')), may hold values from -0.078125 to 0.078125
- residual: bfloat16 [1024, 6144], P('tensor', ('dp', 'side')), may hold values from -1.5 to 1.5
- norm_gain: float32 [6144], replicated, may hold values from 0.1 to 1.9
- router_weight: bfloat16 [6144, 8], replicated, may hold values from -0.02734375 to 0.02734375
- expert_ids: int32 [1024, 2], replicated, may hold values from 0 to 7, all different within a row; in each aligned block of 128 rows (0 to 127, 128 to 255, ...) at most 64 rows name the same one
- gate_weight: bfloat16 [8, 6144, 8192], P('tensor', None, ('dp', 'side')), may hold values from -0.078125 to 0.078125
- up_weight: bfloat16 [8, 6144, 8192], P('tensor', None, ('dp', 'side')), may hold values from -0.078125 to 0.078125
- down_weight: bfloat16 [8, 8192, 6144], P('tensor', ('dp', 'side')), may hold values from -0.0625 to 0.0625
Outputs:
- layer_out: bfloat16 [1024, 6144], P('tensor', ('dp', 'side'))
Inputs may be any that keep to these rules, and one draw needn't show every extreme that they name: `expert_ids`: each row names two different experts; in each aligned block of 128 rows no expert is named by more than 64 rows, and in every draw some expert is named by exactly 64 rows of a block. Row r attends to cached positions 0 to lengths[r] - 1 and to its new key; some rows hold all 192.
All inputs are finite; a program needn't handle non-finite values.
Results may differ from a plain program's by a relative error of at most 0.035.
Values may be sent and summed in bfloat16 or wider, within the bound.
No kernel may reach another device: no remote copies, remote signals or barrier semaphores. Data moves between devices by JAX's collectives and lax.ppermute only.
A program may use at most 128 MiB of HBM per device.

v0:
```python
import jax
import jax.numpy as jnp
from jax import lax
from jax.sharding import PartitionSpec as P

HEAD_DIM = 128
EXPERTS = 8


eps = 1e-05


def slot_tables(expert_ids, experts, blocks, most):
    rows = expert_ids.shape[0]
    block_rows = rows // blocks
    labels = jnp.arange(experts, dtype=jnp.int32)
    chosen = (expert_ids[:, :, None] == labels[None, None, :]).astype(jnp.int32)
    member = jnp.sum(chosen, axis=1)
    ranks = jnp.cumsum(member.reshape(blocks, block_rows, experts), axis=1)
    ranks = ranks.reshape(rows, experts) - 1
    block_of = jnp.arange(rows, dtype=jnp.int32) // block_rows
    slots = block_of[:, None] * most + ranks
    picked = jnp.sum(chosen * slots[:, None, :], axis=2)
    capacity = blocks * most
    row_ids = jnp.broadcast_to(jnp.arange(rows, dtype=jnp.int32)[:, None], (rows, 2))
    others = expert_ids[:, ::-1]
    leads = jnp.broadcast_to(jnp.array([1, 0], dtype=jnp.int32)[None, :], (rows, 2))
    table = jnp.full((experts, capacity), rows, jnp.int32).at[expert_ids, picked].set(row_ids)
    partner = jnp.zeros((experts, capacity), jnp.int32).at[expert_ids, picked].set(others)
    leading = jnp.zeros((experts, capacity), jnp.int32).at[expert_ids, picked].set(leads)
    return (picked, table, partner, leading)


def shards(
    q_new,
    k_new,
    v_new,
    k_cache,
    v_cache,
    lengths,
    attn_out_weight,
    residual,
    norm_gain,
    router_weight,
    expert_ids,
    gate_weight,
    up_weight,
    down_weight,
):
    rows_dev = q_new.shape[0]
    kv_local = k_new.shape[1] // HEAD_DIM
    heads_local = q_new.shape[1] // HEAD_DIM
    group_size = heads_local // kv_local
    cache_len = k_cache.shape[1]
    inv_root = HEAD_DIM ** (-0.5)
    queries = q_new.reshape(rows_dev, kv_local, group_size, HEAD_DIM)
    cache_keys = k_cache.reshape(rows_dev, cache_len, kv_local, HEAD_DIM)
    cache_values = v_cache.reshape(rows_dev, cache_len, kv_local, HEAD_DIM)
    own_keys = k_new.reshape(rows_dev, kv_local, HEAD_DIM)
    own_values = v_new.reshape(rows_dev, kv_local, HEAD_DIM).astype(jnp.float32)
    cache_scores = (
        jnp.einsum("rkgd,rckd->rkgc", queries, cache_keys, preferred_element_type=jnp.float32)
        * inv_root
    )
    own_scores = (
        jnp.einsum("rkgd,rkd->rkg", queries, own_keys, preferred_element_type=jnp.float32)
        * inv_root
    )
    live_mask = (jnp.arange(cache_len, dtype=jnp.int32)[None, :] < lengths[:, None])[
        :, None, None, :
    ]
    cache_scores = jnp.where(live_mask, cache_scores, -1e30)
    peak = jnp.maximum(jnp.max(cache_scores, axis=3), own_scores)
    cache_exp = jnp.exp(cache_scores - peak[..., None])
    own_exp = jnp.exp(own_scores - peak)
    denominator = jnp.sum(cache_exp, axis=3) + own_exp
    cache_weights = (cache_exp / denominator[..., None]).astype(jnp.bfloat16)
    own_weights = (own_exp / denominator).astype(jnp.bfloat16).astype(jnp.float32)
    mixed_heads = jnp.einsum(
        "rkgc,rckd->rkgd", cache_weights, cache_values, preferred_element_type=jnp.float32
    )
    mixed_heads = mixed_heads + own_weights[..., None] * own_values[:, :, None, :]
    attention = mixed_heads.reshape(rows_dev, heads_local * HEAD_DIM).astype(jnp.bfloat16)
    head_sums = jnp.dot(
        lax.all_gather(attention, ("dp", "side"), axis=0, tiled=True),
        attn_out_weight,
        preferred_element_type=jnp.float32,
    )
    total_rows = expert_ids.shape[0]
    tensor_count = lax.axis_size("tensor")
    tensor_rank = lax.axis_index("tensor")
    block_rows = total_rows // tensor_count
    most = block_rows // 2
    experts_local = gate_weight.shape[0]
    col_width = head_sums.shape[1]
    picked, table, partner, leading = slot_tables(expert_ids, EXPERTS, tensor_count, most)
    own_rows = lax.dynamic_slice_in_dim(
        head_sums, tensor_rank * block_rows, block_rows, 0
    ) + residual.astype(jnp.float32)
    head_sums = lax.dynamic_update_slice_in_dim(head_sums, own_rows, tensor_rank * block_rows, 0)
    routed = jnp.take(head_sums, table, axis=0, mode="fill", fill_value=0.0)
    hidden = lax.psum_scatter(
        routed.astype(jnp.bfloat16), "tensor", scatter_dimension=0, tiled=True
    )
    hidden_f = hidden.astype(jnp.float32)
    labels = jnp.arange(EXPERTS, dtype=jnp.int32)
    mine = tensor_rank * experts_local + jnp.arange(experts_local, dtype=jnp.int32)
    features = lax.all_gather(hidden, ("dp", "side"), axis=2, tiled=True).astype(jnp.float32)
    normed = (
        features * lax.rsqrt(jnp.mean(features * features, axis=2, keepdims=True) + eps) * norm_gain
    ).astype(jnp.bfloat16)
    gate = jnp.einsum("ecd,edf->ecf", normed, gate_weight, preferred_element_type=jnp.float32)
    upward = jnp.einsum("ecd,edf->ecf", normed, up_weight, preferred_element_type=jnp.float32)
    logits = jnp.einsum("ecd,dk->eck", normed, router_weight, preferred_element_type=jnp.float32)
    inner = (jax.nn.silu(gate) * upward).astype(jnp.bfloat16)
    summed = lax.psum_scatter(
        jnp.einsum("efd,ecf->dec", down_weight, inner, preferred_element_type=jnp.float32).astype(
            jnp.bfloat16
        ),
        ("dp", "side"),
        scatter_dimension=0,
        tiled=True,
    ).astype(jnp.float32)
    expert_out = jnp.transpose(summed, (1, 2, 0))
    own_logit = jnp.sum(jnp.where(mine[:, None, None] == labels, logits, 0.0), axis=2)
    partner_mine = lax.dynamic_slice_in_dim(partner, tensor_rank * experts_local, experts_local, 0)
    other_logit = jnp.sum(jnp.where(partner_mine[..., None] == labels, logits, 0.0), axis=2)
    shares = jax.nn.sigmoid(own_logit - other_logit)
    parts = (shares[..., None] * expert_out).astype(jnp.bfloat16)
    table_mine = lax.dynamic_slice_in_dim(table, tensor_rank * experts_local, experts_local, 0)
    leading_mine = lax.dynamic_slice_in_dim(leading, tensor_rank * experts_local, experts_local, 0)
    values = parts.astype(jnp.float32) + hidden_f * leading_mine[..., None].astype(jnp.float32)
    buffer = (
        jnp.zeros((total_rows, col_width), jnp.float32)
        .at[table_mine.reshape(-1)]
        .add(values.reshape(-1, col_width), mode="drop")
    )
    out_rows = lax.psum_scatter(
        buffer.astype(jnp.bfloat16), "tensor", scatter_dimension=0, tiled=True
    )
    return out_rows


def solution(mesh):
    return jax.shard_map(
        shards,
        mesh=mesh,
        in_specs=(
            P(("dp", "side"), "tensor"),
            P(("dp", "side"), "tensor"),
            P(("dp", "side"), "tensor"),
            P(("dp", "side"), None, "tensor"),
            P(("dp", "side"), None, "tensor"),
            P(("dp", "side")),
            P("tensor", ("dp", "side")),
            P("tensor", ("dp", "side")),
            P(),
            P(),
            P(),
            P("tensor", None, ("dp", "side")),
            P("tensor", None, ("dp", "side")),
            P("tensor", ("dp", "side"), None),
        ),
        out_specs=P("tensor", ("dp", "side")),
        check_vma=False,
    )
```

profile of v0, /device:TPU:1, one launch (start us, length us, event | category | flops | bytes accessed | tf_op | source)
XLA Modules:
  0.0 370.7 jit_solution(10705472872214771290)
XLA Ops:
  6.5 0.9 iota_compare_fusion.1
  7.4 0.8 convert_element_type.84
  8.2 0.9 reshape.270
  9.1 0.9 fusion.27
  10.0 2.4 fusion.44
  12.6 2.0 fusion.17
  14.7 0.6 copy.56
  15.4 1.0 copy.36
  16.4 2.0 broadcast_add_fusion
  18.4 1.2 copy.37
  19.9 1.0 copy.38
  21.0 1.3 reshape.304
  22.3 0.8 broadcast_in_dim.46
  23.1 1.3 reshape.306
  24.4 8.1 %scatter_custom_fusion.1 = s32[4096]{0:T(1024)S(1)} fusion(s32[2048]{0:T(1024)S(1)} %reshape.304, s32[2048]{0:T(1024)S(1)} %reshape.306, s32[]{:T(128)} %constant.27.clone.1), kind=kCustom, calls=%fused_computation.68 | custom fusion | bytes 16388
  32.6 35.4 %all-gather.3.cloned.1.call-done = bf16[1024,768]{1,0:T(8,128)(2,1)} async-done(((bf16[32,768]{1,0:T(8,128)(2,1)}), bf16[1024,768]{1,0:T(8,128)(2,1)}) %all-gather.3.cloned.1.call-update) | async-done | bytes 1572880 | tf_op jit(solution)/shard_map/all_gather | solution.py:85
  68.0 3.0 fusion.45
  70.9 1.6 add_dynamic-update-slice_fusion
  72.5 2.1 copy.39
  74.6 16.9 %gather_fusion = bf16[4096,192]{1,0:T(8,128)(2,1)} fusion(bf16[1024,192]{1,0:T(8,128)(2,1)} %copy.39, s32[4096]{0:T(1024)S(1)} %broadcast_clamp_fusion), kind=kCustom, calls=%fused_computation | custom fusion | bytes 3162112 | tf_op jit(solution)/shard_map/jit(_take)/gather | solution.py:101
  91.6 3.8 %copy.40 = bf16[8,512,192]{1,2,0:T(8,128)(2,1)} copy(bf16[8,512,192]{2,1,0:T(8,128)(2,1)} %bitcast.68) | data formatting | bytes 3145728 | tf_op jit(solution)/shard_map/jit(_take)/gather | solution.py:101
  95.4 2.9 select_convert_fusion
  98.4 35.6 %reduce-scatter.6.cloned.1.call-done = bf16[1,512,192]{1,2,0:T(8,128)(2,1)} async-done(((bf16[8,512,192]{1,2,0:T(8,128)(2,1)}), bf16[1,512,192]{1,2,0:T(8,128)(2,1)}) %reduce-scatter.6.cloned.1.call-update) | async-done | bytes 196624 | tf_op jit(solution)/shard_map/reduce_scatter | solution.py:102
  134.2 59.3 %all-gather.5.cloned.1.call-done = bf16[1,512,6144]{1,2,0:T(8,128)(2,1)} async-done(((bf16[1,512,192]{1,2,0:T(8,128)(2,1)}), bf16[1,512,6144]{1,2,0:T(8,128)(2,1)}) %all-gather.5.cloned.1.call-update) | async-done | bytes 6291472 | tf_op jit(solution)/shard_map/all_gather | solution.py:108
  193.6 4.3 %fusion = f32[512]{0:T(512)S(1)} fusion(bf16[1,512,6144]{1,2,0:T(8,128)(2,1)} %all-gather.5.cloned.1.call-done), kind=kLoop, calls=%fused_computation.7 | loop fusion | flops 9436672 | bytes 6293504 | tf_op jit(solution)/shard_map/reduce_sum | solution.py:110
  197.9 0.3 copy-done.2
  198.2 1.6 fusion.4
  199.8 2.7 copy-done.1
  202.4 2.6 fusion.8
  205.1 13.1 %fusion.3 = bf16[6144,512]{0,1:T(8,128)(2,1)} fusion(bf16[1,256,6144]{2,1,0:T(8,128)(2,1)S(1)} %copy-done, bf16[512,6144]{0,1:T(8,128)(2,1)} %copy-done.1, bf16[1,6144,256]{2,1,0:T(8,128)(2,1)} %param.27, f32[512,256]{1,0:T(8,128)} %fusion.8), kind=kOutput, calls=%fused_computation.11 | convolution fusion | flops 3225157632 | bytes 19398656 | tf_op jit(solution)/shard_map/efd,ecf->dec/dot_general | solution.py:117
  218.1 8.6 %copy.49 = bf16[6144,512]{1,0:T(8,128)(2,1)} copy(bf16[6144,512]{0,1:T(8,128)(2,1)} %fusion.3) | data formatting | bytes 12582912
  226.8 0.2 rev.3
  227.1 1.1 copy.41
  228.1 1.3 reshape.312
  229.4 8.4 %scatter_custom_fusion.2 = s32[4096]{0:T(1024)S(1)} fusion(s32[2048]{0:T(1024)} %copy-done.9, s32[2048]{0:T(1024)S(1)} %reshape.312, s32[]{:T(128)} %constant.28.clone.1), kind=kCustom, calls=%fused_computation.66 | custom fusion | bytes 16896
  237.9 0.9 broadcast_in_dim.94
  238.8 1.3 reshape.318
  240.1 8.2 %scatter_custom_fusion.3 = s32[4096]{0:T(1024)S(1)} fusion(s32[2048]{0:T(1024)} %copy-done.9, s32[2048]{0:T(1024)S(1)} %reshape.318, s32[]{:T(128)} %constant.28.clone.1), kind=kCustom, calls=%fused_computation.64 | custom fusion | bytes 16896
  248.4 4.0 %select_reduce_fusion.1 = (f32[512]{0:T(512)S(1)}, f32[512]{0:T(512)S(1)}) fusion(s32[512]{0:T(512)S(1)} %bitcast.76, pred[8]{0:T(512)(128)(4,1)S(1)} %iota_compare_fusion.3, bf16[512,6144]{0,1:T(8,128)(2,1)} %copy-done.1, bf16[6144,8]{0,1:T(8,128)(2,1)S(1)} %copy-done.6), kind=kOutput, calls=%fused_computation.50 | convolution fusion | flops 50351104 | bytes 6395912 | tf_op jit(solution)/shard_map/ecd,dk->eck/dot_general | solution.py:114
  252.4 65.5 %reduce-scatter.10.cloned.1.call-done = bf16[192,512]{1,0:T(8,128)(2,1)} async-done(((bf16[6144,512]{1,0:T(8,128)(2,1)}), bf16[192,512]{1,0:T(8,128)(2,1)}) %reduce-scatter.10.cloned.1.call-update) | async-done | bytes 196624
  317.9 1.1 copy.50
  318.9 0.8 copy.42
  319.7 1.1 fusion.22
  320.8 1.0 copy.43
  321.8 4.8 %scatter_custom_fusion = f32[1024,192]{1,0:T(8,128)} fusion(s32[512]{0:T(512)S(1)} %bitcast.78, f32[512,192]{1,0:T(8,128)} %copy.43, f32[]{:T(128)} %constant.25.clone.1), kind=kCustom, calls=%fused_computation.25 | custom fusion | flops 98304 | bytes 786944 | tf_op jit(solution)/shard_map/scatter-add | solution.py:136
  326.6 2.1 convert_element_type.102
  328.7 33.8 %reduce-scatter.8.cloned.1.call-done = bf16[128,192]{1,0:T(8,128)(2,1)} async-done(((bf16[1024,192]{1,0:T(8,128)(2,1)}), bf16[128,192]{1,0:T(8,128)(2,1)}) %reduce-scatter.8.cloned.1.call-update) | async-done | bytes 49168 | tf_op jit(solution)/shard_map/reduce_scatter | solution.py:138
  362.6 1.6 copy.44
  (59 shorter events, 1.1 us)
Async XLA Ops:
  6.5 198.5 %copy-start = (bf16[1,256,6144]{2,1,0:T(8,128)(2,1)S(1)}, bf16[1,256,6144]{2,1,0:T(8,128)(2,1)}, u32[]{:S(2)}) copy-start(bf16[1,256,6144]{2,1,0:T(8,128)(2,1)} %param.28) | copy-start | bytes 9437188
  6.5 8.8 %copy-start.5 = (s32[1024,2]{0,1:T(2,128)S(1)}, s32[1024,2]{0,1:T(2,128)}, u32[]{:S(2)}) copy-start(s32[1024,2]{0,1:T(2,128)} %param.25) | copy-start | bytes 24580
  6.5 61.4 %all-gather.3.cloned.1.call-start = ((), (), s32[]{:S(2)}) async-start(), calls=%async_computation.3 | async-start | bytes 1622016 | tf_op jit(solution)/shard_map/all_gather | solution.py:85
  9.9 9.8 %copy-start.11 = (s32[2]{0:T(128)S(1)}, s32[2]{0:T(128)}, u32[]{:S(2)}) copy-start(s32[2]{0:T(128)} %constant.84) | copy-start | bytes 28
  10.0 9.8 %copy-start.12 = (s32[2]{0:T(128)S(1)}, s32[2]{0:T(128)}, u32[]{:S(2)}) copy-start(s32[2]{0:T(128)} %constant.87) | copy-start | bytes 28
  12.6 55.3 %copy-start.4 = (bf16[768,192]{0,1:T(8,128)(2,1)S(1)}, bf16[768,192]{0,1:T(8,128)(2,1)}, u32[]{:S(2)}) copy-start(bf16[768,192]{0,1:T(8,128)(2,1)} %param.21) | copy-start | bytes 884740
  15.3 118.7 %reduce-scatter.6.cloned.1.call-start = ((), (), s32[]{:S(2)}) async-start(), calls=%async_computation.4 | async-start | bytes 1769472 | tf_op jit(solution)/shard_map/reduce_scatter | solution.py:102
  16.4 54.5 %copy-start.7 = (bf16[128,192]{0,1:T(8,128)(2,1)S(1)}, bf16[128,192]{0,1:T(8,128)(2,1)}, u32[]{:S(2)}) copy-start(bf16[128,192]{0,1:T(8,128)(2,1)} %param.22) | copy-start | bytes 147460
  22.3 2.2 copy-start.9
  98.3 95.2 %all-gather.5.cloned.1.call-start = ((), (), s32[]{:S(2)}) async-start(), calls=%async_computation.5 | async-start | bytes 6488064 | tf_op jit(solution)/shard_map/all_gather | solution.py:108
  134.0 63.9 %copy-start.8 = (f32[6144]{0:T(1024)S(1)}, f32[6144]{0:T(1024)}, u32[]{:S(2)}) copy-start(f32[6144]{0:T(1024)} %param.23) | copy-start | bytes 73732
  134.0 183.8 %reduce-scatter.10.cloned.1.call-start = ((), (), s32[]{:S(2)}) async-start(), calls=%async_computation.7 | async-start | bytes 6488064
  193.6 4.6 %copy-start.2 = (bf16[1,512,6144]{1,2,0:T(8,128)(2,1)S(1)}, bf16[1,512,6144]{1,2,0:T(8,128)(2,1)}, u32[]{:S(2)}) copy-start(bf16[1,512,6144]{1,2,0:T(8,128)(2,1)} %all-gather.5.cloned.1.call-done) | copy-start | bytes 18874372
  198.2 4.3 %copy-start.3 = (bf16[1,6144,256]{2,1,0:T(8,128)(2,1)S(1)}, bf16[1,6144,256]{2,1,0:T(8,128)(2,1)}, u32[]{:S(2)}) copy-start(bf16[1,6144,256]{2,1,0:T(8,128)(2,1)} %param.26) | copy-start | bytes 9437188
  199.8 2.7 copy-start.1
  226.8 11.1 %copy-start.10 = (s32[2]{0:T(128)S(1)}, s32[2]{0:T(128)}, u32[]{:S(2)}) copy-start(s32[2]{0:T(128)} %constant.80.clone) | copy-start | bytes 28
  226.8 21.6 %copy-start.6 = (bf16[6144,8]{0,1:T(8,128)(2,1)S(1)}, bf16[6144,8]{0,1:T(8,128)(2,1)}, u32[]{:S(2)}) copy-start(bf16[6144,8]{0,1:T(8,128)(2,1)} %param.24) | copy-start | bytes 294916
  226.8 135.8 %reduce-scatter.8.cloned.1.call-start = ((), (), s32[]{:S(2)}) async-start(), calls=%async_computation.6 | async-start | bytes 589824 | tf_op jit(solution)/shard_map/reduce_scatter | solution.py:138
Sparse Core Ops, SparseCore 0:
  15.4 52.4 all-gather.2
  98.4 35.4 reduce-scatter.5
  136.5 56.9 all-gather.4
  226.9 90.8 reduce-scatter.9
  328.9 33.6 reduce-scatter.7
where the time goes:
time: 376 us; the launch traced here: 371 us
  waiting for transfers between devices  230 us (61%)
  local copies, waits for them, and re-layouts  76.7 us (20%)
  matrix products  27.9 us (7%)
  other arithmetic  22.5 us (6%)
  between operations  13.5 us (4%)
    unnamed x6, waiting for transfers between devices  65.6 us
    all_gather x1, waiting for transfers between devices, shards(): lax.all_gather(hidden, ('dp', 'side'), axis=2, tiled=True)  59.3 us
    unnamed x35, local copies, waits for them, and re-layouts  40.4 us
    reduce_scatter x1, waiting for transfers between devices, shards(): lax.psum_scatter(routed.astype(jnp.bfloat16), 'tensor', scatter_dimension...  35.6 us
    all_gather x1, waiting for transfers between devices, shards(): lax.all_gather(attention, ('dp', 'side'), axis=0, tiled=True)  35.4 us
    reduce_scatter x1, waiting for transfers between devices, shards(): lax.psum_scatter(buffer.astype(jnp.bfloat16), 'tensor', scatter_dimension...  33.8 us
    gather x2, local copies, waits for them, and re-layouts, shards(): routed = jnp.take(head_sums, table, axis=0, mode='fill', fill_value=0.0)  20.8 us
    dot_general x1, matrix products, shards(): jnp.einsum('efd,ecf->dec', down_weight, inner, preferred_element_type=jnp...  13.1 us
  transfers between devices with their start and end apart: 5, of which 5 were waited for; matrix products, arithmetic and copies ran while one was open for 11% of the time, Pallas kernels for 0%

commit v1 on v0

v1 whole, which is shorter than its diff:
```python
import jax
import jax.numpy as jnp
from jax import lax
from jax.experimental import pallas as pl
from jax.experimental.pallas import tpu as pltpu
from jax.sharding import PartitionSpec as P

HEAD_DIM = 128
EXPERTS = 8
eps = 1e-05
F32 = jnp.float32
BF16 = jnp.bfloat16
VMEM_LIMIT = 48 * 1024 * 1024

SHIFT_X = [[(4 * x + y, 4 * ((x + d) % 4) + y) for x in range(4) for y in range(4)] for d in range(4)]
SHIFT_Y = [[(4 * x + y, 4 * x + (y + d) % 4) for x in range(4) for y in range(4)] for d in range(4)]
SWAP = [(0, 1), (1, 0)]


def swap_cores(a):
    return lax.ppermute(a, "side", SWAP)


def gather_xy(a, b):
    a_in = [lax.ppermute(a, "dp", SHIFT_X[d]) for d in (1, 2, 3)]
    b_in = [lax.ppermute(b, "dp", SHIFT_Y[d]) for d in (1, 2, 3)]
    ga = jnp.stack([a] + a_in)
    gb = jnp.stack([b] + b_in)
    first = [ga] + [lax.ppermute(ga, "dp", SHIFT_Y[d]) for d in (1, 2, 3)]
    second = [gb] + [lax.ppermute(gb, "dp", SHIFT_X[d]) for d in (1, 2, 3)]
    return first, second


def outproj_kernel(pos, own, other, w, out):
    x, y, c = pos[0], pos[1], pos[2]
    for ref, side in ((own, c), (other, 1 - c)):
        for h in range(2):
            sums = jnp.dot(
                ref[h].reshape(256, 768), w[...], preferred_element_type=F32
            ).astype(BF16)
            for k in range(16):
                dx, dy = (k % 4, k // 4) if h == 0 else (k // 4, k % 4)
                chip = ((x - dx) & 3) * 4 + ((y - dy) & 3)
                row = pl.multiple_of((chip * 2 + side) * 32 + h * 16, 16)
                out[pl.ds(row, 16), :] = sums[k * 16 : k * 16 + 16]


def norm_kernel(pos, a0, a1, a2, a3, b0, b1, b2, b3, gain, out):
    x, y = pos[0], pos[1]
    for h, refs in ((0, (a0, a1, a2, a3)), (1, (b0, b1, b2, b3))):
        for r0 in range(0, 128, 32):
            squares = jnp.zeros((32, 384), F32)
            for i in range(4):
                for j in range(4):
                    v = refs[i][j, r0 : r0 + 32, :].astype(F32)
                    squares = squares + v * v
            mean = jnp.sum(squares, axis=1, keepdims=True) * (1.0 / 6144.0)
            scale = lax.rsqrt(mean + eps)
            for i in range(4):
                for j in range(4):
                    dx, dy = (j, i) if h == 0 else (i, j)
                    chip = ((x - dx) & 3) * 4 + ((y - dy) & 3)
                    v = refs[i][j, r0 : r0 + 32, :].astype(F32)
                    out[chip, h * 128 + r0 : h * 128 + r0 + 32, :] = (
                        v * scale * gain[chip]
                    ).astype(BF16)


def expert_kernel(xn, gate_w, up_w, router, inner, logits, gate, up, logit):
    k = pl.program_id(0)

    @pl.when(k == 0)
    def _():
        gate[...] = jnp.zeros_like(gate)
        up[...] = jnp.zeros_like(up)
        logit[...] = jnp.zeros_like(logit)

    for j in range(4):
        rows = slice(j * 384, j * 384 + 384)
        v = xn[j]
        gate[...] += jnp.dot(v, gate_w[rows, :], preferred_element_type=F32)
        up[...] += jnp.dot(v, up_w[rows, :], preferred_element_type=F32)
        logit[...] += jnp.dot(v, router[rows, :], preferred_element_type=F32)

    @pl.when(k == pl.num_programs(0) - 1)
    def _():
        g = gate[...]
        inner[...] = (g / (1.0 + jnp.exp(-g)) * up[...]).astype(BF16)
        logits[...] = logit[...]


def expert_call(xn, gate_w, up_w, router):
    return pl.pallas_call(
        expert_kernel,
        grid=(4,),
        in_specs=[
            pl.BlockSpec((4, 256, 384), lambda k: (k, 0, 0)),
            pl.BlockSpec((1536, 256), lambda k: (k, 0)),
            pl.BlockSpec((1536, 256), lambda k: (k, 0)),
            pl.BlockSpec((1536, EXPERTS), lambda k: (k, 0)),
        ],
        out_specs=[
            pl.BlockSpec((256, 256), lambda k: (0, 0)),
            pl.BlockSpec((256, EXPERTS), lambda k: (0, 0)),
        ],
        out_shape=[
            jax.ShapeDtypeStruct((256, 256), BF16),
            jax.ShapeDtypeStruct((256, EXPERTS), F32),
        ],
        scratch_shapes=[
            pltpu.VMEM((256, 256), F32),
            pltpu.VMEM((256, 256), F32),
            pltpu.VMEM((256, EXPERTS), F32),
        ],
        compiler_params=pltpu.CompilerParams(vmem_limit_bytes=VMEM_LIMIT),
        name="expert_in",
    )(xn, gate_w, up_w, router)


def down_kernel(pos, inner, w, out_a, out_b):
    sums = jnp.dot(inner[...], w[...], preferred_element_type=F32).astype(BF16)
    out_a[0, 0] = sums[:128]
    out_b[0, 0] = sums[128:]


def down_call(pos, inner, down_w):
    return pl.pallas_call(
        down_kernel,
        grid_spec=pltpu.PrefetchScalarGridSpec(
            num_scalar_prefetch=1,
            grid=(4, 4),
            in_specs=[
                pl.BlockSpec((256, 256), lambda i, j, pos: (0, 0)),
                pl.BlockSpec(
                    (256, 384),
                    lambda i, j, pos: (0, ((pos[0] + j) & 3) * 4 + ((pos[1] + i) & 3)),
                ),
            ],
            out_specs=[
                pl.BlockSpec((1, 1, 128, 384), lambda i, j, pos: (i, j, 0, 0)),
                pl.BlockSpec((1, 1, 128, 384), lambda i, j, pos: (j, i, 0, 0)),
            ],
        ),
        out_shape=[jax.ShapeDtypeStruct((4, 4, 128, 384), BF16)] * 2,
        compiler_params=pltpu.CompilerParams(vmem_limit_bytes=VMEM_LIMIT),
        name="expert_down",
    )(pos, inner, down_w)


def attend(q_new, k_new, v_new, k_cache, v_cache, lengths):
    rows_dev = q_new.shape[0]
    kv_local = k_new.shape[1] // HEAD_DIM
    heads_local = q_new.shape[1] // HEAD_DIM
    group_size = heads_local // kv_local
    cache_len = k_cache.shape[1]
    inv_root = HEAD_DIM ** (-0.5)
    queries = q_new.reshape(rows_dev, kv_local, group_size, HEAD_DIM)
    cache_keys = k_cache.reshape(rows_dev, cache_len, kv_local, HEAD_DIM)
    cache_values = v_cache.reshape(rows_dev, cache_len, kv_local, HEAD_DIM)
    own_keys = k_new.reshape(rows_dev, kv_local, HEAD_DIM)
    own_values = v_new.reshape(rows_dev, kv_local, HEAD_DIM).astype(F32)
    cache_scores = (
        jnp.einsum("rkgd,rckd->rkgc", queries, cache_keys, preferred_element_type=F32) * inv_root
    )
    own_scores = (
        jnp.einsum("rkgd,rkd->rkg", queries, own_keys, preferred_element_type=F32) * inv_root
    )
    live_mask = (jnp.arange(cache_len, dtype=jnp.int32)[None, :] < lengths[:, None])[
        :, None, None, :
    ]
    cache_scores = jnp.where(live_mask, cache_scores, -1e30)
    peak = jnp.maximum(jnp.max(cache_scores, axis=3), own_scores)
    cache_exp = jnp.exp(cache_scores - peak[..., None])
    own_exp = jnp.exp(own_scores - peak)
    denominator = jnp.sum(cache_exp, axis=3) + own_exp
    cache_weights = (cache_exp / denominator[..., None]).astype(BF16)
    own_weights = (own_exp / denominator).astype(BF16).astype(F32)
    mixed_heads = jnp.einsum(
        "rkgc,rckd->rkgd", cache_weights, cache_values, preferred_element_type=F32
    )
    mixed_heads = mixed_heads + own_weights[..., None] * own_values[:, :, None, :]
    return mixed_heads.reshape(rows_dev, heads_local * HEAD_DIM).astype(BF16)


def ranks_of(member):
    n = member.shape[0]
    lower = (
        lax.broadcasted_iota(jnp.int32, (n, n), 0) >= lax.broadcasted_iota(jnp.int32, (n, n), 1)
    ).astype(BF16)
    counts = jnp.dot(lower, member.astype(BF16), preferred_element_type=F32).astype(jnp.int32)
    return jnp.where(member, counts - 1, -1)


def shards(
    q_new,
    k_new,
    v_new,
    k_cache,
    v_cache,
    lengths,
    attn_out_weight,
    residual,
    norm_gain,
    router_weight,
    expert_ids,
    gate_weight,
    up_weight,
    down_weight,
):
    chip = lax.axis_index("dp")
    core = lax.axis_index("side")
    plane = lax.axis_index("tensor")
    pos = jnp.stack([chip // 4, chip % 4, core]).astype(jnp.int32)
    first_core = core == 0

    labels = jnp.arange(EXPERTS, dtype=jnp.int32)
    block_ids = lax.dynamic_slice_in_dim(expert_ids, plane * 128, 128, 0)
    member = jnp.any(block_ids[:, :, None] == labels, axis=1)
    ranks = ranks_of(member).T
    slots = jnp.arange(32, dtype=jnp.int32)
    pick_own = (ranks[:, None, :] - core * 32 == slots[:, None]).astype(BF16).reshape(256, 128)
    pick_other = (
        (ranks[:, None, :] - (1 - core) * 32 == slots[:, None]).astype(BF16).reshape(256, 128)
    )
    ids_by_block = expert_ids.reshape(8, 128, 2)
    named = jnp.any(ids_by_block == plane, axis=2)
    ranks_mine = ranks_of(named.T).T
    partner_ids = jnp.sum(ids_by_block, axis=2) - plane
    hits = ranks_mine[:, None, :] - core * 32 == slots[:, None]
    partner = jnp.sum(jnp.where(hits, partner_ids[:, None, :], 0), axis=2).reshape(256, 1)
    signs = (labels == plane).astype(F32) - (labels == partner).astype(F32)

    attention = attend(q_new, k_new, v_new, k_cache, v_cache, lengths)
    first, second = gather_xy(attention[:16], attention[16:])
    rows_own = jnp.stack(
        [jnp.concatenate(first, axis=0), jnp.concatenate(second, axis=0)]
    )
    rows_other = swap_cores(rows_own)
    head_sums = pl.pallas_call(
        outproj_kernel,
        in_specs=[pl.BlockSpec(memory_space=pltpu.SMEM)]
        + [pl.BlockSpec(memory_space=pltpu.VMEM)] * 3,
        out_specs=pl.BlockSpec(memory_space=pltpu.VMEM),
        out_shape=jax.ShapeDtypeStruct((1024, 192), BF16),
        compiler_params=pltpu.CompilerParams(vmem_limit_bytes=VMEM_LIMIT),
        name="out_projection",
    )(pos, rows_own, rows_other, attn_out_weight)
    heads_in = lax.all_to_all(
        head_sums.reshape(8, 128, 192), "tensor", split_axis=0, concat_axis=0, tiled=True
    )
    hidden = (jnp.sum(heads_in.astype(F32), axis=0) + residual.astype(F32)).astype(BF16)
    hidden_other = swap_cores(hidden)
    hidden_chip = jnp.where(
        first_core,
        jnp.concatenate([hidden, hidden_other], axis=1),
        jnp.concatenate([hidden_other, hidden], axis=1),
    )
    routed = jnp.dot(pick_own, hidden_chip, preferred_element_type=F32).astype(BF16)
    mine = lax.all_to_all(
        routed.reshape(8, 32, 384), "tensor", split_axis=0, concat_axis=0, tiled=True
    ).reshape(256, 384)

    first, second = gather_xy(mine[:128], mine[128:])
    normed = pl.pallas_call(
        norm_kernel,
        in_specs=[pl.BlockSpec(memory_space=pltpu.SMEM)]
        + [pl.BlockSpec(memory_space=pltpu.VMEM)] * 9,
        out_specs=pl.BlockSpec(memory_space=pltpu.VMEM),
        out_shape=jax.ShapeDtypeStruct((16, 256, 384), BF16),
        compiler_params=pltpu.CompilerParams(vmem_limit_bytes=VMEM_LIMIT),
        name="norm",
    )(pos, *first, *second, norm_gain.reshape(16, 1, 384))
    normed_other = swap_cores(normed)
    gate_w, up_w, down_w = gate_weight[0], up_weight[0], down_weight[0]
    inner_own, logits = expert_call(normed, gate_w, up_w, router_weight)
    inner_other, _ = expert_call(normed_other, gate_w, up_w, router_weight)
    shares = jax.nn.sigmoid(jnp.sum(logits * signs, axis=1, keepdims=True))
    other_a, other_b = down_call(pos, inner_other, down_w)
    in_a, in_b = swap_cores(other_a), swap_cores(other_b)
    own_a, own_b = down_call(pos, inner_own, down_w)

    def add(*terms):
        total = terms[0].astype(F32)
        for term in terms[1:]:
            total = total + term.astype(F32)
        return total

    part_a = [add(own_a[d], in_a[d]) for d in range(4)]
    part_b = [add(own_b[d], in_b[d]) for d in range(4)]
    got_a = [lax.ppermute(part_a[d].astype(BF16), "dp", SHIFT_Y[d]) for d in (1, 2, 3)]
    got_b = [lax.ppermute(part_b[d].astype(BF16), "dp", SHIFT_X[d]) for d in (1, 2, 3)]
    row_a = add(part_a[0], *got_a)
    row_b = add(part_b[0], *got_b)
    got_a = [lax.ppermute(row_a[d].astype(BF16), "dp", SHIFT_X[d]) for d in (1, 2, 3)]
    got_b = [lax.ppermute(row_b[d].astype(BF16), "dp", SHIFT_Y[d]) for d in (1, 2, 3)]
    expert_out = jnp.concatenate([add(row_a[0], *got_a), add(row_b[0], *got_b)], axis=0)

    parts = (shares * expert_out).astype(BF16)
    back = lax.all_to_all(
        parts.reshape(8, 32, 384), "tensor", split_axis=0, concat_axis=0, tiled=True
    ).reshape(256, 384)
    keep = jnp.where(first_core, back[:, :192], back[:, 192:])
    give = jnp.where(first_core, back[:, 192:], back[:, :192])
    taken = swap_cores(give)

    def spread(pick, rows):
        return lax.dot_general(
            pick, rows, (((0,), (0,)), ((), ())), preferred_element_type=F32
        )

    return (
        hidden.astype(F32) + spread(pick_own, keep) + spread(pick_other, taken)
    ).astype(BF16)


def solution(mesh):
    return jax.shard_map(
        shards,
        mesh=mesh,
        in_specs=(
            P(("dp", "side"), "tensor"),
            P(("dp", "side"), "tensor"),
            P(("dp", "side"), "tensor"),
            P(("dp", "side"), None, "tensor"),
            P(("dp", "side"), None, "tensor"),
            P(("dp", "side")),
            P("tensor", ("dp", "side")),
            P("tensor", ("dp", "side")),
            P(),
            P(),
            P(),
            P("tensor", None, ("dp", "side")),
            P("tensor", None, ("dp", "side")),
            P("tensor", ("dp", "side"), None),
        ),
        out_specs=P("tensor", ("dp", "side")),
        check_vma=False,
    )
```

time: 376 us -> 236 us (0.63)
  waiting for transfers between devices: 230 us -> 71.6 us
  starting transfers between devices: 0.35 us -> 74.9 us
  local copies, waits for them, and re-layouts: 76.7 us -> 5.78 us
  Pallas kernels: 0 us -> 40.2 us
  blocking collectives: 0 us -> 24.2 us
  matrix products: 27.9 us -> 4.09 us
  between operations: 13.5 us -> 0.7 us
  other arithmetic: 22.5 us -> 10.1 us
    all_gather x2 -> x0, waiting for transfers between devices: 94.7 us -> none  [the longest x1 59.3 us: shards(): lax.all_gather(hidden, ('dp', 'side'), axis=2, tiled=True)]
    reduce_scatter x2 -> x0, waiting for transfers between devices: 69.4 us -> none  [the longest x1 35.6 us: shards(): lax.psum_scatter(routed.astype(jnp.bfloat16), 'tensor', scatter_dimension...]
    ppermute x0 -> x42, starting transfers between devices: none -> 66.7 us  [the longest x6 22 us: swap_cores(): return lax.ppermute(a, 'side', SWAP)]
    unnamed x6 -> x0, waiting for transfers between devices: 65.6 us -> none
    ppermute x0 -> x42, waiting for transfers between devices: none -> 56.5 us  [the longest x3 14.7 us: shards(): lax.ppermute(part_a[d].astype(BF16), 'dp', SHIFT_Y[d])]
    pallas_call x0 -> x6, Pallas kernels: none -> 40.2 us  [the longest x2 21.8 us: down_call(): pl.pallas_call(down_kernel, grid_spec=pltpu.PrefetchScalarGridSpec(num_sc...]
    unnamed x35 -> x46, local copies, waits for them, and re-layouts: 40.4 us -> 3.33 us
    all_to_all x0 -> x2, blocking collectives: none -> 24.2 us  [the longest x1 13.4 us: shards(): lax.all_to_all(routed.reshape(8, 32, 384), 'tensor', split_axis=0, concat...]
  transfers between devices with their start and end apart: 5 -> 43, of which waited for: 5 -> 24; matrix products, arithmetic and copies ran while one was open for 11% -> 5% of each run, Pallas kernels for 0% -> 7%
where the time goes in v1:
time: 236 us; the launch traced here: 232 us
  starting transfers between devices  74.9 us (32%)
  waiting for transfers between devices  71.6 us (30%)
  Pallas kernels  40.2 us (17%)
  blocking collectives  24.2 us (10%)
  other arithmetic  10.1 us (4%)
  local copies, waits for them, and re-layouts  5.78 us (2%)
  matrix products  4.09 us (2%)
    ppermute x6, starting transfers between devices, swap_cores(): return lax.ppermute(a, 'side', SWAP)  22 us
    pallas_call x2, Pallas kernels, down_call(): pl.pallas_call(down_kernel, grid_spec=pltpu.PrefetchScalarGridSpec(num_sc...  21.8 us
    all_to_all x1, waiting for transfers between devices, shards(): lax.all_to_all(head_sums.reshape(8, 128, 192), 'tensor', split_axis=0, co...  15.1 us
    ppermute x3, waiting for transfers between devices, shards(): lax.ppermute(part_a[d].astype(BF16), 'dp', SHIFT_Y[d])  14.7 us
    all_to_all x1, blocking collectives, shards(): lax.all_to_all(routed.reshape(8, 32, 384), 'tensor', split_axis=0, concat...  13.4 us
    pallas_call x2, Pallas kernels, expert_call(): pl.pallas_call(expert_kernel, grid=(4,), in_specs=[pl.BlockSpec((4, 256,...  12.7 us
    ppermute x6, waiting for transfers between devices, gather_xy(): first = [ga] + [lax.ppermute(ga, 'dp', SHIFT_Y[d]) for d in (1, 2, 3)]  11.2 us
    all_to_all x1, blocking collectives, shards(): lax.all_to_all(parts.reshape(8, 32, 384), 'tensor', split_axis=0, concat_...  10.8 us
  transfers between devices with their start and end apart: 43, of which 24 were waited for; matrix products, arithmetic and copies ran while one was open for 5% of the time, Pallas kernels for 7%

profile of v1, /device:TPU:1, one launch (start us, length us, event | category | flops | bytes accessed | tf_op | source)
XLA Modules:
  0.0 231.6 jit_solution(2774197237000549533)
XLA Ops:
  4.5 2.1 collective-permute-start
  6.6 2.5 %collective-permute-start.1 = (bf16[16,768]{1,0:T(8,128)(2,1)S(1)}, bf16[16,768]{1,0:T(8,128)(2,1)S(1)}, u32[]{:S(2)}, u32[]{:S(2)}) collective-permute-start(bf16[16,768]{1,0:T(8,128)(2,1)S(1)} %bitcast.162), channel_id=1, source_target_pairs={{0,128},{16,144},{32,160},{48,176},{64,192},{80,208},{96,224},{112... | collective-permute-start | bytes 73736 | tf_op jit(solution)/shard_map/ppermute | solution.py:25
  9.1 1.2 collective-permute-start.2
  10.2 1.3 collective-permute-start.6
  11.5 2.6 %collective-permute-start.7 = (bf16[16,768]{1,0:T(8,128)(2,1)S(1)}, bf16[16,768]{1,0:T(8,128)(2,1)S(1)}, u32[]{:S(2)}, u32[]{:S(2)}) collective-permute-start(bf16[16,768]{1,0:T(8,128)(2,1)S(1)} %bitcast.159), channel_id=1, source_target_pairs={{0,32},{16,48},{32,0},{48,16},{64,96},{80,112},{96,64},{112,80},{1... | collective-permute-start | bytes 73736 | tf_op jit(solution)/shard_map/ppermute | solution.py:26
  16.8 1.7 collective-permute-start.5
  18.9 1.6 collective-permute-start.10
  21.9 2.4 %collective-permute-done.9 = bf16[4,16,768]{2,1,0:T(8,128)(2,1)S(1)} collective-permute-done((bf16[4,16,768]{2,1,0:T(8,128)(2,1)S(1)}, bf16[4,16,768]{2,1,0:T(8,128)(2,1)S(1)}, u32[]{:S(2)}, u32[]{:S(2)}) %collective-permute-start.9) | collective-permute-done | bytes 98336 | tf_op jit(solution)/shard_map/ppermute | solution.py:30
  25.3 4.1 %collective-permute-start.12 = (bf16[2,16,16,768]{3,2,1,0:T(8,128)(2,1)S(1)}, bf16[2,16,16,768]{3,2,1,0:T(8,128)(2,1)}, u32[]{:S(2)}, u32[]{:S(2)}) collective-permute-start(bf16[2,16,16,768]{3,2,1,0:T(8,128)(2,1)S(1)} %pad_maximum_fusion.own), channel_id=1, source_target_pairs={{0,1},{1,0},{2,3},{3,2},{4,5},{5,4},{6,7},{7,6},{8,9},{9,8},{10,11... | collective-permute-start | bytes 2359304 | tf_op jit(solution)/shard_map/ppermute | solution.py:21
  29.7 1.8 collective-permute-done.12.other
  31.5 1.7 out_projection.1
  34.1 8.2 %all-to-all-start = ((bf16[8,128,192]{1,2,0:T(8,128)(2,1)}), bf16[8,128,192]{1,2,0:T(8,128)(2,1)S(1)}, u32[]{:S(2)}, u32[]{:S(2)}) async-start(bf16[8,128,192]{1,2,0:T(8,128)(2,1)} %copy.31), calls=%async_computation | async-start | bytes 786432 | tf_op jit(solution)/shard_map/all_to_all | solution.py:248
  42.4 15.1 %all-to-all-done = bf16[8,128,192]{1,2,0:T(8,128)(2,1)S(1)} async-done(((bf16[8,128,192]{1,2,0:T(8,128)(2,1)}), bf16[8,128,192]{1,2,0:T(8,128)(2,1)S(1)}, u32[]{:S(2)}, u32[]{:S(2)}) %all-to-all-start) | async-done | bytes 393248 | tf_op jit(solution)/shard_map/all_to_all | solution.py:248
  60.0 13.4 %all_to_all.15 = bf16[8,32,384]{2,1,0:T(8,128)(2,1)S(1)} all-to-all(bf16[8,32,384]{2,1,0:T(8,128)(2,1)S(1)} %bitcast.143), channel_id=1, replica_groups=mesh['dp'=16,'tensor'=8,'side'=2] {'tensor'}, dimensions={0} | all-to-all | bytes 393216 | tf_op jit(solution)/shard_map/all_to_all | solution.py:259
  73.9 2.2 collective-permute-start.21
  76.0 2.0 collective-permute-start.22
  78.8 1.8 collective-permute-done.21
  82.0 3.0 %collective-permute-start.15 = (bf16[128,384]{1,0:T(8,128)(2,1)S(1)}, bf16[128,384]{1,0:T(8,128)(2,1)S(1)}, u32[]{:S(2)}, u32[]{:S(2)}) collective-permute-start(bf16[128,384]{1,0:T(8,128)(2,1)S(1)} %bitcast.134), channel_id=1, source_target_pairs={{0,128},{16,144},{32,160},{48,176},{64,192},{80,208},{96,224},{112... | collective-permute-start | bytes 294920 | tf_op jit(solution)/shard_map/ppermute | solution.py:25
  85.0 1.7 collective-permute-start.16
  87.0 6.5 %collective-permute-done.14 = bf16[128,384]{1,0:T(8,128)(2,1)S(1)} collective-permute-done((bf16[128,384]{1,0:T(8,128)(2,1)S(1)}, bf16[128,384]{1,0:T(8,128)(2,1)S(1)}, u32[]{:S(2)}, u32[]{:S(2)}) %collective-permute-start.14) | collective-permute-done | bytes 98336 | tf_op jit(solution)/shard_map/ppermute | solution.py:25
  94.6 1.5 collective-permute-done.15
  96.2 2.9 %collective-permute-start.17 = (bf16[4,128,384]{2,1,0:T(8,128)(2,1)S(1)}, bf16[4,128,384]{2,1,0:T(8,128)(2,1)S(1)}, u32[]{:S(2)}, u32[]{:S(2)}) collective-permute-start(bf16[4,128,384]{2,1,0:T(8,128)(2,1)S(1)} %pad_maximum_fusion.1.a0), channel_id=1, source_target_pairs={{0,16},{16,32},{32,48},{48,0},{64,80},{80,96},{96,112},{112,64},{1... | collective-permute-start | bytes 1179656 | tf_op jit(solution)/shard_map/ppermute | solution.py:29
  99.1 1.9 collective-permute-start.18
  101.6 3.2 %collective-permute-done.24.b2 = bf16[4,128,384]{2,1,0:T(8,128)(2,1)S(1)} collective-permute-done((bf16[4,128,384]{2,1,0:T(8,128)(2,1)S(1)}, bf16[4,128,384]{2,1,0:T(8,128)(2,1)S(1)}, u32[]{:S(2)}, u32[]{:S(2)}) %collective-permute-start.24) | collective-permute-done | bytes 393248 | tf_op jit(solution)/shard_map/ppermute | solution.py:30
  105.5 8.6 %collective-permute-done.18.a2 = bf16[4,128,384]{2,1,0:T(8,128)(2,1)S(1)} collective-permute-done((bf16[4,128,384]{2,1,0:T(8,128)(2,1)S(1)}, bf16[4,128,384]{2,1,0:T(8,128)(2,1)S(1)}, u32[]{:S(2)}, u32[]{:S(2)}) %collective-permute-start.18) | collective-permute-done | bytes 393248 | tf_op jit(solution)/shard_map/ppermute | solution.py:29
  114.2 1.9 collective-permute-done.19.a3
  116.0 4.1 %norm.1.xn = bf16[16,256,384]{2,1,0:T(8,128)(2,1)} custom-call(s32[3]{0:T(128)S(1)} %pad_add_fusion.pos, bf16[4,128,384]{2,1,0:T(8,128)(2,1)S(1)} %pad_maximum_fusion.1.a0, bf16[4,128,384]{2,1,0:T(8,128)(2,1)S(1)} %collective-permute-done.17.a1, bf16[4,128,384]{2,1,0:T(8,128)(2,1)S(1)} %collective-permute-done.18.a2, ...), custom_call_target="tpu_custom_call" | custom-call | tf_op jit(solution)/shard_map/norm/pallas_call | solution.py:264
  120.1 13.4 %collective-permute-start.26 = (bf16[16,256,384]{2,1,0:T(8,128)(2,1)}, bf16[16,256,384]{2,1,0:T(8,128)(2,1)}, u32[]{:S(2)}, u32[]{:S(2)}) collective-permute-start(bf16[16,256,384]{2,1,0:T(8,128)(2,1)} %norm.1.xn), channel_id=1, source_target_pairs={{0,1},{1,0},{2,3},{3,2},{4,5},{5,4},{6,7},{7,6},{8,9},{9,8},{10,11... | collective-permute-start | bytes 9437192 | tf_op jit(solution)/shard_map/ppermute | solution.py:21
  134.3 4.8 %collective-permute-done.26.xn = bf16[16,256,384]{2,1,0:T(8,128)(2,1)} collective-permute-done((bf16[16,256,384]{2,1,0:T(8,128)(2,1)}, bf16[16,256,384]{2,1,0:T(8,128)(2,1)}, u32[]{:S(2)}, u32[]{:S(2)}) %collective-permute-start.26) | collective-permute-done | bytes 3145760 | tf_op jit(solution)/shard_map/ppermute | solution.py:21
  139.2 6.9 %expert_in.3 = (bf16[256,256]{1,0:T(8,128)(2,1)S(1)}, f32[256,8]{1,0:T(8,128)}) custom-call(bf16[16,256,384]{2,1,0:T(8,128)(2,1)} %collective-permute-done.26.xn, bf16[6144,256]{1,0:T(8,128)(2,1)} %bitcast.124, bf16[6144,256]{1,0:T(8,128)(2,1)} %bitcast.126, bf16[6144,8]{1,0:T(8,128)(2,1)S(1)} %copy.34.router), custom_call_target="tpu_custom_call" | custom-call | tf_op jit(solution)/shard_map/expert_in/pallas_call | solution.py:93
  146.1 11.6 %expert_down.3 = (bf16[4,4,128,384]{3,2,1,0:T(8,128)(2,1)}, bf16[4,4,128,384]{3,2,1,0:T(8,128)(2,1)}) custom-call(s32[3]{0:T(128)S(1)} %pad_add_fusion.pos, bf16[256,256]{1,0:T(8,128)(2,1)S(1)} %get-tuple-element.15.inner, bf16[256,6144]{1,0:T(8,128)(2,1)} %bitcast.122), custom_call_target="tpu_custom_call" | custom-call | tf_op jit(solution)/shard_map/expert_down/pallas_call | solution.py:127
  158.7 1.9 copy-done.1
  160.6 5.8 %expert_in.2 = (bf16[256,256]{1,0:T(8,128)(2,1)S(1)}, f32[256,8]{1,0:T(8,128)S(1)}) custom-call(bf16[16,256,384]{2,1,0:T(8,128)(2,1)S(1)} %copy-done.1, bf16[6144,256]{1,0:T(8,128)(2,1)} %bitcast.125, bf16[6144,256]{1,0:T(8,128)(2,1)} %bitcast.127, bf16[6144,8]{1,0:T(8,128)(2,1)S(1)} %copy.34.router), custom_call_target="tpu_custom_call" | custom-call | tf_op jit(solution)/shard_map/expert_in/pallas_call | solution.py:93
  166.3 10.2 %expert_down.2 = (bf16[4,4,128,384]{3,2,1,0:T(8,128)(2,1)S(1)}, bf16[4,4,128,384]{3,2,1,0:T(8,128)(2,1)S(1)}) custom-call(s32[3]{0:T(128)S(1)} %pad_add_fusion.pos, bf16[256,256]{1,0:T(8,128)(2,1)S(1)} %get-tuple-element.13.inner, bf16[256,6144]{1,0:T(8,128)(2,1)} %bitcast.123), custom_call_target="tpu_custom_call" | custom-call | tf_op jit(solution)/shard_map/expert_down/pallas_call | solution.py:127
  176.8 2.8 %fusion.12 = (bf16[4,128,384]{2,1,0:T(8,128)(2,1)}, bf16[4,128,384]{2,1,0:T(8,128)(2,1)}, bf16[4,128,384]{2,1,0:T(8,128)(2,1)}) fusion(bf16[4,4,128,384]{3,2,1,0:T(8,128)(2,1)} %collective-permute-done.27, bf16[4,4,128,384]{3,2,1,0:T(8,128)(2,1)S(1)} %get-tuple-element.14), kind=kLoop, calls=%fused_computation.29 | loop fusion | flops 2359296 | bytes 3538944 | tf_op jit(solution)/shard_map/convert_element_type | solution.py:290
  180.6 2.1 collective-permute-start.29
  183.6 1.6 fusion.15
  185.6 5.7 %collective-permute-done.28 = bf16[4,128,384]{2,1,0:T(8,128)(2,1)S(1)} collective-permute-done((bf16[4,128,384]{2,1,0:T(8,128)(2,1)}, bf16[4,128,384]{2,1,0:T(8,128)(2,1)S(1)}, u32[]{:S(2)}, u32[]{:S(2)}) %collective-permute-start.28) | collective-permute-done | bytes 393248 | tf_op jit(solution)/shard_map/ppermute | solution.py:290
  191.4 8.9 %collective-permute-done.29 = bf16[4,128,384]{2,1,0:T(8,128)(2,1)} collective-permute-done((bf16[4,128,384]{2,1,0:T(8,128)(2,1)}, bf16[4,128,384]{2,1,0:T(8,128)(2,1)}, u32[]{:S(2)}, u32[]{:S(2)}) %collective-permute-start.29) | collective-permute-done | bytes 393248 | tf_op jit(solution)/shard_map/ppermute | solution.py:290
  200.3 1.6 fusion.44
  202.4 2.0 collective-permute-done.35
  205.5 1.2 fusion.46
  206.8 1.4 collective-permute-start.38
  208.2 2.3 %collective-permute-start.39 = (bf16[128,384]{1,0:T(8,128)(2,1)S(1)}, bf16[128,384]{1,0:T(8,128)(2,1)S(1)}, u32[]{:S(2)}, u32[]{:S(2)}) collective-permute-start(bf16[128,384]{1,0:T(8,128)(2,1)S(1)} %get-tuple-element.34), channel_id=1, source_target_pairs={{0,32},{16,48},{32,0},{48,16},{64,96},{80,112},{96,64},{112,80},{1... | collective-permute-start | bytes 294920 | tf_op jit(solution)/shard_map/ppermute | solution.py:295
  210.5 2.4 %collective-permute-start.40 = (bf16[128,384]{1,0:T(8,128)(2,1)S(1)}, bf16[128,384]{1,0:T(8,128)(2,1)S(1)}, u32[]{:S(2)}, u32[]{:S(2)}) collective-permute-start(bf16[128,384]{1,0:T(8,128)(2,1)S(1)} %get-tuple-element.33), channel_id=1, source_target_pairs={{0,48},{16,0},{32,16},{48,32},{64,112},{80,64},{96,80},{112,96},{1... | collective-permute-start | bytes 294920 | tf_op jit(solution)/shard_map/ppermute | solution.py:295
  214.1 1.3 collective-permute-done.40
  215.6 10.8 %all_to_all.16 = bf16[8,32,384]{2,1,0:T(8,128)(2,1)S(1)} all-to-all(bf16[8,32,384]{2,1,0:T(8,128)(2,1)S(1)} %multiply_convert_fusion), channel_id=1, replica_groups=mesh['dp'=16,'tensor'=8,'side'=2] {'tensor'}, dimensions={0} | all-to-all | bytes 393216 | tf_op jit(solution)/shard_map/all_to_all | solution.py:299
  226.5 3.1 %collective-permute-start.41 = (bf16[256,192]{1,0:T(8,128)(2,1)S(1)}, bf16[256,192]{1,0:T(8,128)(2,1)S(1)}, u32[]{:S(2)}, u32[]{:S(2)}) collective-permute-start(bf16[256,192]{1,0:T(8,128)(2,1)S(1)} %broadcast_select_fusion), channel_id=1, source_target_pairs={{0,1},{1,0},{2,3},{3,2},{4,5},{5,4},{6,7},{7,6},{8,9},{9,8},{10,11... | collective-permute-start | bytes 294920 | tf_op jit(solution)/shard_map/ppermute | solution.py:21
  (146 shorter events, 28.1 us)
Async XLA Ops:
  4.5 9.8 %collective-permute-start = (bf16[16,768]{1,0:T(8,128)(2,1)S(1)}, bf16[16,768]{1,0:T(8,128)(2,1)S(1)}, u32[]{:S(2)}, u32[]{:S(2)}) collective-permute-start(bf16[16,768]{1,0:T(8,128)(2,1)S(1)} %bitcast.161), channel_id=1, source_target_pairs={{0,64},{16,80},{32,96},{48,112},{64,128},{80,144},{96,160},{112,17... | collective-permute-start | bytes 73736 | tf_op jit(solution)/shard_map/ppermute | solution.py:25
  6.6 8.8 %collective-permute-start.1 = (bf16[16,768]{1,0:T(8,128)(2,1)S(1)}, bf16[16,768]{1,0:T(8,128)(2,1)S(1)}, u32[]{:S(2)}, u32[]{:S(2)}) collective-permute-start(bf16[16,768]{1,0:T(8,128)(2,1)S(1)} %bitcast.162), channel_id=1, source_target_pairs={{0,128},{16,144},{32,160},{48,176},{64,192},{80,208},{96,224},{112... | collective-permute-start | bytes 73736 | tf_op jit(solution)/shard_map/ppermute | solution.py:25
  9.1 6.4 %collective-permute-start.2 = (bf16[16,768]{1,0:T(8,128)(2,1)S(1)}, bf16[16,768]{1,0:T(8,128)(2,1)S(1)}, u32[]{:S(2)}, u32[]{:S(2)}) collective-permute-start(bf16[16,768]{1,0:T(8,128)(2,1)S(1)} %bitcast.163), channel_id=1, source_target_pairs={{0,192},{16,208},{32,224},{48,240},{64,0},{80,16},{96,32},{112,48}... | collective-permute-start | bytes 73736 | tf_op jit(solution)/shard_map/ppermute | solution.py:25
  10.2 6.5 %collective-permute-start.6 = (bf16[16,768]{1,0:T(8,128)(2,1)S(1)}, bf16[16,768]{1,0:T(8,128)(2,1)S(1)}, u32[]{:S(2)}, u32[]{:S(2)}) collective-permute-start(bf16[16,768]{1,0:T(8,128)(2,1)S(1)} %bitcast.158), channel_id=1, source_target_pairs={{0,16},{16,32},{32,48},{48,0},{64,80},{80,96},{96,112},{112,64},{1... | collective-permute-start | bytes 73736 | tf_op jit(solution)/shard_map/ppermute | solution.py:26
  11.5 6.9 %collective-permute-start.7 = (bf16[16,768]{1,0:T(8,128)(2,1)S(1)}, bf16[16,768]{1,0:T(8,128)(2,1)S(1)}, u32[]{:S(2)}, u32[]{:S(2)}) collective-permute-start(bf16[16,768]{1,0:T(8,128)(2,1)S(1)} %bitcast.159), channel_id=1, source_target_pairs={{0,32},{16,48},{32,0},{48,16},{64,96},{80,112},{96,64},{112,80},{1... | collective-permute-start | bytes 73736 | tf_op jit(solution)/shard_map/ppermute | solution.py:26
  14.3 4.2 %collective-permute-start.8 = (bf16[16,768]{1,0:T(8,128)(2,1)S(1)}, bf16[16,768]{1,0:T(8,128)(2,1)S(1)}, u32[]{:S(2)}, u32[]{:S(2)}) collective-permute-start(bf16[16,768]{1,0:T(8,128)(2,1)S(1)} %bitcast.160), channel_id=1, source_target_pairs={{0,48},{16,0},{32,16},{48,32},{64,112},{80,64},{96,80},{112,96},{1... | collective-permute-start | bytes 73736 | tf_op jit(solution)/shard_map/ppermute | solution.py:26
  15.5 5.4 %collective-permute-start.3 = (bf16[4,16,768]{2,1,0:T(8,128)(2,1)S(1)}, bf16[4,16,768]{2,1,0:T(8,128)(2,1)S(1)}, u32[]{:S(2)}, u32[]{:S(2)}) collective-permute-start(bf16[4,16,768]{2,1,0:T(8,128)(2,1)S(1)} %pad_maximum_fusion.4), channel_id=1, source_target_pairs={{0,16},{16,32},{32,48},{48,0},{64,80},{80,96},{96,112},{112,64},{1... | collective-permute-start | bytes 294920 | tf_op jit(solution)/shard_map/ppermute | solution.py:29
  16.0 5.7 %collective-permute-start.4 = (bf16[4,16,768]{2,1,0:T(8,128)(2,1)S(1)}, bf16[4,16,768]{2,1,0:T(8,128)(2,1)S(1)}, u32[]{:S(2)}, u32[]{:S(2)}) collective-permute-start(bf16[4,16,768]{2,1,0:T(8,128)(2,1)S(1)} %pad_maximum_fusion.4), channel_id=1, source_target_pairs={{0,32},{16,48},{32,0},{48,16},{64,96},{80,112},{96,64},{112,80},{1... | collective-permute-start | bytes 294920 | tf_op jit(solution)/shard_map/ppermute | solution.py:29
  16.8 5.1 %collective-permute-start.5 = (bf16[4,16,768]{2,1,0:T(8,128)(2,1)S(1)}, bf16[4,16,768]{2,1,0:T(8,128)(2,1)S(1)}, u32[]{:S(2)}, u32[]{:S(2)}) collective-permute-start(bf16[4,16,768]{2,1,0:T(8,128)(2,1)S(1)} %pad_maximum_fusion.4), channel_id=1, source_target_pairs={{0,48},{16,0},{32,16},{48,32},{64,112},{80,64},{96,80},{112,96},{1... | collective-permute-start | bytes 294920 | tf_op jit(solution)/shard_map/ppermute | solution.py:29
  18.5 5.9 %collective-permute-start.9 = (bf16[4,16,768]{2,1,0:T(8,128)(2,1)S(1)}, bf16[4,16,768]{2,1,0:T(8,128)(2,1)S(1)}, u32[]{:S(2)}, u32[]{:S(2)}) collective-permute-start(bf16[4,16,768]{2,1,0:T(8,128)(2,1)S(1)} %pad_maximum_fusion.5), channel_id=1, source_target_pairs={{0,64},{16,80},{32,96},{48,112},{64,128},{80,144},{96,160},{112,17... | collective-permute-start | bytes 294920 | tf_op jit(solution)/shard_map/ppermute | solution.py:30
  18.9 5.5 %collective-permute-start.10 = (bf16[4,16,768]{2,1,0:T(8,128)(2,1)S(1)}, bf16[4,16,768]{2,1,0:T(8,128)(2,1)S(1)}, u32[]{:S(2)}, u32[]{:S(2)}) collective-permute-start(bf16[4,16,768]{2,1,0:T(8,128)(2,1)S(1)} %pad_maximum_fusion.5), channel_id=1, source_target_pairs={{0,128},{16,144},{32,160},{48,176},{64,192},{80,208},{96,224},{112... | collective-permute-start | bytes 294920 | tf_op jit(solution)/shard_map/ppermute | solution.py:30
  20.9 4.3 %collective-permute-start.11 = (bf16[4,16,768]{2,1,0:T(8,128)(2,1)S(1)}, bf16[4,16,768]{2,1,0:T(8,128)(2,1)S(1)}, u32[]{:S(2)}, u32[]{:S(2)}) collective-permute-start(bf16[4,16,768]{2,1,0:T(8,128)(2,1)S(1)} %pad_maximum_fusion.5), channel_id=1, source_target_pairs={{0,192},{16,208},{32,224},{48,240},{64,0},{80,16},{96,32},{112,48}... | collective-permute-start | bytes 294920 | tf_op jit(solution)/shard_map/ppermute | solution.py:30
  25.3 6.1 %collective-permute-start.12 = (bf16[2,16,16,768]{3,2,1,0:T(8,128)(2,1)S(1)}, bf16[2,16,16,768]{3,2,1,0:T(8,128)(2,1)}, u32[]{:S(2)}, u32[]{:S(2)}) collective-permute-start(bf16[2,16,16,768]{3,2,1,0:T(8,128)(2,1)S(1)} %pad_maximum_fusion.own), channel_id=1, source_target_pairs={{0,1},{1,0},{2,3},{3,2},{4,5},{5,4},{6,7},{7,6},{8,9},{9,8},{10,11... | collective-permute-start | bytes 2359304 | tf_op jit(solution)/shard_map/ppermute | solution.py:21
  33.2 24.4 %copy-start.7 = (bf16[128,192]{0,1:T(8,128)(2,1)S(1)}, bf16[128,192]{0,1:T(8,128)(2,1)}, u32[]{:S(2)}) copy-start(bf16[128,192]{0,1:T(8,128)(2,1)} %param.21) | copy-start | bytes 147460
  34.1 23.4 %all-to-all-start = ((bf16[8,128,192]{1,2,0:T(8,128)(2,1)}), bf16[8,128,192]{1,2,0:T(8,128)(2,1)S(1)}, u32[]{:S(2)}, u32[]{:S(2)}) async-start(bf16[8,128,192]{1,2,0:T(8,128)(2,1)} %copy.31), calls=%async_computation | async-start | bytes 786432 | tf_op jit(solution)/shard_map/all_to_all | solution.py:248
  57.6 58.4 %copy-start.3 = (f32[6144]{0:T(1024)S(1)}, f32[6144]{0:T(1024)}, u32[]{:S(2)}) copy-start(f32[6144]{0:T(1024)} %param.22) | copy-start | bytes 73732
  57.6 1.8 collective-permute-start.13
  73.4 5.4 %collective-permute-start.20 = (bf16[128,384]{1,0:T(8,128)(2,1)S(1)}, bf16[128,384]{1,0:T(8,128)(2,1)S(1)}, u32[]{:S(2)}, u32[]{:S(2)}) collective-permute-start(bf16[128,384]{1,0:T(8,128)(2,1)S(1)} %bitcast.137), channel_id=1, source_target_pairs={{0,16},{16,32},{32,48},{48,0},{64,80},{80,96},{96,112},{112,64},{1... | collective-permute-start | bytes 294920 | tf_op jit(solution)/shard_map/ppermute | solution.py:26
  73.9 6.7 %collective-permute-start.21 = (bf16[128,384]{1,0:T(8,128)(2,1)S(1)}, bf16[128,384]{1,0:T(8,128)(2,1)S(1)}, u32[]{:S(2)}, u32[]{:S(2)}) collective-permute-start(bf16[128,384]{1,0:T(8,128)(2,1)S(1)} %bitcast.138), channel_id=1, source_target_pairs={{0,32},{16,48},{32,0},{48,16},{64,96},{80,112},{96,64},{112,80},{1... | collective-permute-start | bytes 294920 | tf_op jit(solution)/shard_map/ppermute | solution.py:26
  76.0 5.0 %collective-permute-start.22 = (bf16[128,384]{1,0:T(8,128)(2,1)S(1)}, bf16[128,384]{1,0:T(8,128)(2,1)S(1)}, u32[]{:S(2)}, u32[]{:S(2)}) collective-permute-start(bf16[128,384]{1,0:T(8,128)(2,1)S(1)} %bitcast.139), channel_id=1, source_target_pairs={{0,48},{16,0},{32,16},{48,32},{64,112},{80,64},{96,80},{112,96},{1... | collective-permute-start | bytes 294920 | tf_op jit(solution)/shard_map/ppermute | solution.py:26
  81.1 19.9 %collective-permute-start.23 = (bf16[4,128,384]{2,1,0:T(8,128)(2,1)S(1)}, bf16[4,128,384]{2,1,0:T(8,128)(2,1)S(1)}, u32[]{:S(2)}, u32[]{:S(2)}) collective-permute-start(bf16[4,128,384]{2,1,0:T(8,128)(2,1)S(1)} %pad_maximum_fusion.2.b0), channel_id=1, source_target_pairs={{0,64},{16,80},{32,96},{48,112},{64,128},{80,144},{96,160},{112,17... | collective-permute-start | bytes 1179656 | tf_op jit(solution)/shard_map/ppermute | solution.py:30
  81.9 11.5 %collective-permute-start.14 = (bf16[128,384]{1,0:T(8,128)(2,1)S(1)}, bf16[128,384]{1,0:T(8,128)(2,1)S(1)}, u32[]{:S(2)}, u32[]{:S(2)}) collective-permute-start(bf16[128,384]{1,0:T(8,128)(2,1)S(1)} %bitcast.133), channel_id=1, source_target_pairs={{0,64},{16,80},{32,96},{48,112},{64,128},{80,144},{96,160},{112,17... | collective-permute-start | bytes 294920 | tf_op jit(solution)/shard_map/ppermute | solution.py:25
  82.0 14.1 %collective-permute-start.15 = (bf16[128,384]{1,0:T(8,128)(2,1)S(1)}, bf16[128,384]{1,0:T(8,128)(2,1)S(1)}, u32[]{:S(2)}, u32[]{:S(2)}) collective-permute-start(bf16[128,384]{1,0:T(8,128)(2,1)S(1)} %bitcast.134), channel_id=1, source_target_pairs={{0,128},{16,144},{32,160},{48,176},{64,192},{80,208},{96,224},{112... | collective-permute-start | bytes 294920 | tf_op jit(solution)/shard_map/ppermute | solution.py:25
  85.0 11.1 %collective-permute-start.16 = (bf16[128,384]{1,0:T(8,128)(2,1)S(1)}, bf16[128,384]{1,0:T(8,128)(2,1)S(1)}, u32[]{:S(2)}, u32[]{:S(2)}) collective-permute-start(bf16[128,384]{1,0:T(8,128)(2,1)S(1)} %bitcast.135), channel_id=1, source_target_pairs={{0,192},{16,208},{32,224},{48,240},{64,0},{80,16},{96,32},{112,48}... | collective-permute-start | bytes 294920 | tf_op jit(solution)/shard_map/ppermute | solution.py:25
  86.7 18.1 %collective-permute-start.24 = (bf16[4,128,384]{2,1,0:T(8,128)(2,1)S(1)}, bf16[4,128,384]{2,1,0:T(8,128)(2,1)S(1)}, u32[]{:S(2)}, u32[]{:S(2)}) collective-permute-start(bf16[4,128,384]{2,1,0:T(8,128)(2,1)S(1)} %pad_maximum_fusion.2.b0), channel_id=1, source_target_pairs={{0,128},{16,144},{32,160},{48,176},{64,192},{80,208},{96,224},{112... | collective-permute-start | bytes 1179656 | tf_op jit(solution)/shard_map/ppermute | solution.py:30
  93.5 12.0 %collective-permute-start.25 = (bf16[4,128,384]{2,1,0:T(8,128)(2,1)S(1)}, bf16[4,128,384]{2,1,0:T(8,128)(2,1)S(1)}, u32[]{:S(2)}, u32[]{:S(2)}) collective-permute-start(bf16[4,128,384]{2,1,0:T(8,128)(2,1)S(1)} %pad_maximum_fusion.2.b0), channel_id=1, source_target_pairs={{0,192},{16,208},{32,224},{48,240},{64,0},{80,16},{96,32},{112,48}... | collective-permute-start | bytes 1179656 | tf_op jit(solution)/shard_map/ppermute | solution.py:30
  96.2 9.3 %collective-permute-start.17 = (bf16[4,128,384]{2,1,0:T(8,128)(2,1)S(1)}, bf16[4,128,384]{2,1,0:T(8,128)(2,1)S(1)}, u32[]{:S(2)}, u32[]{:S(2)}) collective-permute-start(bf16[4,128,384]{2,1,0:T(8,128)(2,1)S(1)} %pad_maximum_fusion.1.a0), channel_id=1, source_target_pairs={{0,16},{16,32},{32,48},{48,0},{64,80},{80,96},{96,112},{112,64},{1... | collective-permute-start | bytes 1179656 | tf_op jit(solution)/shard_map/ppermute | solution.py:29
  99.1 15.0 %collective-permute-start.18 = (bf16[4,128,384]{2,1,0:T(8,128)(2,1)S(1)}, bf16[4,128,384]{2,1,0:T(8,128)(2,1)S(1)}, u32[]{:S(2)}, u32[]{:S(2)}) collective-permute-start(bf16[4,128,384]{2,1,0:T(8,128)(2,1)S(1)} %pad_maximum_fusion.1.a0), channel_id=1, source_target_pairs={{0,32},{16,48},{32,0},{48,16},{64,96},{80,112},{96,64},{112,80},{1... | collective-permute-start | bytes 1179656 | tf_op jit(solution)/shard_map/ppermute | solution.py:29
  101.0 15.0 %collective-permute-start.19 = (bf16[4,128,384]{2,1,0:T(8,128)(2,1)S(1)}, bf16[4,128,384]{2,1,0:T(8,128)(2,1)S(1)}, u32[]{:S(2)}, u32[]{:S(2)}) collective-permute-start(bf16[4,128,384]{2,1,0:T(8,128)(2,1)S(1)} %pad_maximum_fusion.1.a0), channel_id=1, source_target_pairs={{0,48},{16,0},{32,16},{48,32},{64,112},{80,64},{96,80},{112,96},{1... | collective-permute-start | bytes 1179656 | tf_op jit(solution)/shard_map/ppermute | solution.py:29
  116.0 17.5 %copy-start.6 = (bf16[6144,8]{0,1:T(8,128)(2,1)S(1)}, bf16[6144,8]{0,1:T(8,128)(2,1)}, u32[]{:S(2)}) copy-start(bf16[6144,8]{0,1:T(8,128)(2,1)} %param.23) | copy-start | bytes 294916
  120.1 19.1 %collective-permute-start.26 = (bf16[16,256,384]{2,1,0:T(8,128)(2,1)}, bf16[16,256,384]{2,1,0:T(8,128)(2,1)}, u32[]{:S(2)}, u32[]{:S(2)}) collective-permute-start(bf16[16,256,384]{2,1,0:T(8,128)(2,1)} %norm.1.xn), channel_id=1, source_target_pairs={{0,1},{1,0},{2,3},{3,2},{4,5},{5,4},{6,7},{7,6},{8,9},{9,8},{10,11... | collective-permute-start | bytes 9437192 | tf_op jit(solution)/shard_map/ppermute | solution.py:21
  157.6 19.1 %collective-permute-start.27 = (bf16[4,4,128,384]{3,2,1,0:T(8,128)(2,1)}, bf16[4,4,128,384]{3,2,1,0:T(8,128)(2,1)}, u32[]{:S(2)}, u32[]{:S(2)}) collective-permute-start(bf16[4,4,128,384]{3,2,1,0:T(8,128)(2,1)} %get-tuple-element.16), channel_id=1, source_target_pairs={{0,1},{1,0},{2,3},{3,2},{4,5},{5,4},{6,7},{7,6},{8,9},{9,8},{10,11... | collective-permute-start | bytes 4718600 | tf_op jit(solution)/shard_map/ppermute | solution.py:21
  158.0 25.6 %collective-permute-start.34 = (bf16[4,4,128,384]{3,2,1,0:T(8,128)(2,1)}, bf16[4,4,128,384]{3,2,1,0:T(8,128)(2,1)}, u32[]{:S(2)}, u32[]{:S(2)}) collective-permute-start(bf16[4,4,128,384]{3,2,1,0:T(8,128)(2,1)} %get-tuple-element.18), channel_id=1, source_target_pairs={{0,1},{1,0},{2,3},{3,2},{4,5},{5,4},{6,7},{7,6},{8,9},{9,8},{10,11... | collective-permute-start | bytes 4718600 | tf_op jit(solution)/shard_map/ppermute | solution.py:21
  179.6 11.8 %collective-permute-start.28 = (bf16[4,128,384]{2,1,0:T(8,128)(2,1)}, bf16[4,128,384]{2,1,0:T(8,128)(2,1)S(1)}, u32[]{:S(2)}, u32[]{:S(2)}) collective-permute-start(bf16[4,128,384]{2,1,0:T(8,128)(2,1)} %get-tuple-element.23), channel_id=1, source_target_pairs={{0,16},{16,32},{32,48},{48,0},{64,80},{80,96},{96,112},{112,64},{1... | collective-permute-start | bytes 1179656 | tf_op jit(solution)/shard_map/ppermute | solution.py:290
  180.6 19.7 %collective-permute-start.29 = (bf16[4,128,384]{2,1,0:T(8,128)(2,1)}, bf16[4,128,384]{2,1,0:T(8,128)(2,1)}, u32[]{:S(2)}, u32[]{:S(2)}) collective-permute-start(bf16[4,128,384]{2,1,0:T(8,128)(2,1)} %get-tuple-element.25), channel_id=1, source_target_pairs={{0,32},{16,48},{32,0},{48,16},{64,96},{80,112},{96,64},{112,80},{1... | collective-permute-start | bytes 1179656 | tf_op jit(solution)/shard_map/ppermute | solution.py:290
  182.7 17.6 %collective-permute-start.30 = (bf16[4,128,384]{2,1,0:T(8,128)(2,1)}, bf16[4,128,384]{2,1,0:T(8,128)(2,1)}, u32[]{:S(2)}, u32[]{:S(2)}) collective-permute-start(bf16[4,128,384]{2,1,0:T(8,128)(2,1)} %get-tuple-element.24), channel_id=1, source_target_pairs={{0,48},{16,0},{32,16},{48,32},{64,112},{80,64},{96,80},{112,96},{1... | collective-permute-start | bytes 1179656 | tf_op jit(solution)/shard_map/ppermute | solution.py:290
  185.2 19.1 %collective-permute-start.35 = (bf16[4,128,384]{2,1,0:T(8,128)(2,1)S(1)}, bf16[4,128,384]{2,1,0:T(8,128)(2,1)S(1)}, u32[]{:S(2)}, u32[]{:S(2)}) collective-permute-start(bf16[4,128,384]{2,1,0:T(8,128)(2,1)S(1)} %get-tuple-element.26), channel_id=1, source_target_pairs={{0,64},{16,80},{32,96},{48,112},{64,128},{80,144},{96,160},{112,17... | collective-permute-start | bytes 1179656 | tf_op jit(solution)/shard_map/ppermute | solution.py:291
  185.3 19.4 %collective-permute-start.36 = (bf16[4,128,384]{2,1,0:T(8,128)(2,1)S(1)}, bf16[4,128,384]{2,1,0:T(8,128)(2,1)S(1)}, u32[]{:S(2)}, u32[]{:S(2)}) collective-permute-start(bf16[4,128,384]{2,1,0:T(8,128)(2,1)S(1)} %get-tuple-element.28), channel_id=1, source_target_pairs={{0,128},{16,144},{32,160},{48,176},{64,192},{80,208},{96,224},{112... | collective-permute-start | bytes 1179656 | tf_op jit(solution)/shard_map/ppermute | solution.py:291
  191.4 14.1 %collective-permute-start.37 = (bf16[4,128,384]{2,1,0:T(8,128)(2,1)S(1)}, bf16[4,128,384]{2,1,0:T(8,128)(2,1)S(1)}, u32[]{:S(2)}, u32[]{:S(2)}) collective-permute-start(bf16[4,128,384]{2,1,0:T(8,128)(2,1)S(1)} %get-tuple-element.27), channel_id=1, source_target_pairs={{0,192},{16,208},{32,224},{48,240},{64,0},{80,16},{96,32},{112,48}... | collective-permute-start | bytes 1179656 | tf_op jit(solution)/shard_map/ppermute | solution.py:291
  201.9 8.6 %collective-permute-start.31 = (bf16[128,384]{1,0:T(8,128)(2,1)S(1)}, bf16[128,384]{1,0:T(8,128)(2,1)S(1)}, u32[]{:S(2)}, u32[]{:S(2)}) collective-permute-start(bf16[128,384]{1,0:T(8,128)(2,1)S(1)} %get-tuple-element.29), channel_id=1, source_target_pairs={{0,64},{16,80},{32,96},{48,112},{64,128},{80,144},{96,160},{112,17... | collective-permute-start | bytes 294920 | tf_op jit(solution)/shard_map/ppermute | solution.py:294
  202.0 10.9 %collective-permute-start.32 = (bf16[128,384]{1,0:T(8,128)(2,1)S(1)}, bf16[128,384]{1,0:T(8,128)(2,1)S(1)}, u32[]{:S(2)}, u32[]{:S(2)}) collective-permute-start(bf16[128,384]{1,0:T(8,128)(2,1)S(1)} %get-tuple-element.31), channel_id=1, source_target_pairs={{0,128},{16,144},{32,160},{48,176},{64,192},{80,208},{96,224},{112... | collective-permute-start | bytes 294920 | tf_op jit(solution)/shard_map/ppermute | solution.py:294
  204.3 8.6 %collective-permute-start.33 = (bf16[128,384]{1,0:T(8,128)(2,1)S(1)}, bf16[128,384]{1,0:T(8,128)(2,1)S(1)}, u32[]{:S(2)}, u32[]{:S(2)}) collective-permute-start(bf16[128,384]{1,0:T(8,128)(2,1)S(1)} %get-tuple-element.30), channel_id=1, source_target_pairs={{0,192},{16,208},{32,224},{48,240},{64,0},{80,16},{96,32},{112,48}... | collective-permute-start | bytes 294920 | tf_op jit(solution)/shard_map/ppermute | solution.py:294
  206.8 6.2 %collective-permute-start.38 = (bf16[128,384]{1,0:T(8,128)(2,1)S(1)}, bf16[128,384]{1,0:T(8,128)(2,1)S(1)}, u32[]{:S(2)}, u32[]{:S(2)}) collective-permute-start(bf16[128,384]{1,0:T(8,128)(2,1)S(1)} %get-tuple-element.32), channel_id=1, source_target_pairs={{0,16},{16,32},{32,48},{48,0},{64,80},{80,96},{96,112},{112,64},{1... | collective-permute-start | bytes 294920 | tf_op jit(solution)/shard_map/ppermute | solution.py:295
  208.2 5.9 %collective-permute-start.39 = (bf16[128,384]{1,0:T(8,128)(2,1)S(1)}, bf16[128,384]{1,0:T(8,128)(2,1)S(1)}, u32[]{:S(2)}, u32[]{:S(2)}) collective-permute-start(bf16[128,384]{1,0:T(8,128)(2,1)S(1)} %get-tuple-element.34), channel_id=1, source_target_pairs={{0,32},{16,48},{32,0},{48,16},{64,96},{80,112},{96,64},{112,80},{1... | collective-permute-start | bytes 294920 | tf_op jit(solution)/shard_map/ppermute | solution.py:295
  210.5 4.8 %collective-permute-start.40 = (bf16[128,384]{1,0:T(8,128)(2,1)S(1)}, bf16[128,384]{1,0:T(8,128)(2,1)S(1)}, u32[]{:S(2)}, u32[]{:S(2)}) collective-permute-start(bf16[128,384]{1,0:T(8,128)(2,1)S(1)} %get-tuple-element.33), channel_id=1, source_target_pairs={{0,48},{16,0},{32,16},{48,32},{64,112},{80,64},{96,80},{112,96},{1... | collective-permute-start | bytes 294920 | tf_op jit(solution)/shard_map/ppermute | solution.py:295
  213.0 16.6 %copy-start.9 = (bf16[128,192]{0,1:T(8,128)(2,1)S(1)}, bf16[128,192]{0,1:T(8,128)(2,1)}, u32[]{:S(2)}) copy-start(bf16[128,192]{0,1:T(8,128)(2,1)} %copy-done.8) | copy-start | bytes 147460
  213.0 16.6 %copy-start.12 = (pred[256,128]{1,0:T(32,128)(4,1)S(1)}, pred[256,128]{1,0:T(32,128)(4,1)}, u32[]{:S(2)}) copy-start(pred[256,128]{1,0:T(32,128)(4,1)} %copy-done.11) | copy-start | bytes 98308
  226.5 4.1 %collective-permute-start.41 = (bf16[256,192]{1,0:T(8,128)(2,1)S(1)}, bf16[256,192]{1,0:T(8,128)(2,1)S(1)}, u32[]{:S(2)}, u32[]{:S(2)}) collective-permute-start(bf16[256,192]{1,0:T(8,128)(2,1)S(1)} %broadcast_select_fusion), channel_id=1, source_target_pairs={{0,1},{1,0},{2,3},{3,2},{4,5},{5,4},{6,7},{7,6},{8,9},{9,8},{10,11... | collective-permute-start | bytes 294920 | tf_op jit(solution)/shard_map/ppermute | solution.py:21
  (10 other events, 56.9 us)
